TPU v7x, 32 devices: a whole 2x2x4 slice. The times are simulated.
32 devices in a mesh: pipe: 2 (over x), dp: 4 (over y, core), tensor: 4 (over z).
Axes of the slice: x: 2, y: 2, z: 4, core: 2. Of those that a mesh axis runs over, the one named last changes fastest.
Arguments:
- inputs: bfloat16 [4, 1024, 1024], P(None, ('dp', 'tensor')), may hold values from -6 to 6
- segments: int32 [4, 1024], P(None, 'dp'), may hold values from 0 to 7, never falling along the last dimension, each value on 1 to 256 neighbouring positions
- cotangent: bfloat16 [4, 1024, 1024], P(None, ('dp', 'tensor')), may hold values from -6 to 6
- w_qkv: bfloat16 [2, 1024, 3, 1024], P('pipe', 'dp', None, 'tensor'), may hold values from -0.1875 to 0.1875
- w_o: bfloat16 [2, 1024, 1024], P('pipe', 'tensor', 'dp'), may hold values from -1.5 to 1.5
- w_in: bfloat16 [2, 1024, 4096], P('pipe', 'dp', 'tensor'), may hold values from -0.1875 to 0.1875
- w_out: bfloat16 [2, 4096, 1024], P('pipe', 'tensor', 'dp'), may hold values from -0.09375 to 0.09375
- ln_gains: float32 [2, 2, 1024], P('pipe'), may hold values from 0.1 to 1.9
- model_biases: float32 [2, 6, 1024], P('pipe'), may hold values from -1 to 1
- hidden_bias: float32 [2, 4096], P('pipe'), may hold values from -2.5 to 2.5
Outputs:
- section_outputs: bfloat16 [2, 4, 1024, 1024], P('pipe', None, ('dp', 'tensor'))
- input_grads: bfloat16 [2, 4, 1024, 1024], P('pipe', None, ('dp', 'tensor'))
- grad_qkv: float32 [2, 1024, 3, 1024], P('pipe', 'dp', None, 'tensor')
- grad_o: float32 [2, 1024, 1024], P('pipe', 'tensor', 'dp')
- grad_in: float32 [2, 1024, 4096], P('pipe', 'dp', 'tensor')
- grad_out: float32 [2, 4096, 1024], P('pipe', 'tensor', 'dp')
- grad_gains: float32 [2, 2, 1024], P('pipe', None, ('dp', 'tensor'))
- grad_biases: float32 [2, 6, 1024], P('pipe', None, ('dp', 'tensor'))
- grad_hidden_bias: float32 [2, 4096], P('pipe', ('dp', 'tensor'))
Inputs may be any that keep to these rules, and one draw needn't show every extreme that they name: `segments`: segment numbers never fall along a micro-batch's 1024 tokens; a segment holds 1 to 256 tokens and some segment holds exactly 256.
All inputs are finite; a program needn't handle non-finite values.
Results may differ from a plain program's by a relative error of at most 0.028.
Values may be sent and summed in bfloat16 or wider, within the bound.
No kernel may reach another device: no remote copies, remote signals or barrier semaphores. Data moves between devices by JAX's collectives and lax.ppermute only.
A program may use at most 128 MiB of HBM per device.

v0:
```python
import jax
import jax.numpy as jnp
from jax import lax
from jax.sharding import PartitionSpec as P

HEAD_DIM = 64
NORM_EPS = 1e-12
MASKED = -1000000000.0
ROOT_HALF = 0.7071067811865476
INV_ROOT_TWOPI = 0.3989422804014327


def shifted(block, axis, distance):
    devices = range(lax.axis_size(axis))
    route = [(i - distance, i) for i in devices if i - distance in devices]
    return lax.ppermute(block, axis, route)


def dot_rows(left_side, right_side):
    return lax.dot_general(
        left_side, right_side, (((0,), (0,)), ((), ())), preferred_element_type=jnp.float32
    )


def dot_cols(left_side, right_side):
    return lax.dot_general(
        left_side, right_side, (((1,), (1,)), ((), ())), preferred_element_type=jnp.float32
    )


def norm_forward(values, gain_row, shift_row):
    center = values - jnp.mean(values, axis=-1, keepdims=True)
    spread = jnp.mean(center * center, axis=-1, keepdims=True)
    inverse = lax.rsqrt(spread + NORM_EPS)
    scaled = center * inverse
    return (scaled * gain_row + shift_row, scaled, inverse)


def norm_backward(upstream, scaled, inverse, gain_row):
    weighted = upstream * gain_row
    inner_term = (
        weighted
        - jnp.mean(weighted, axis=-1, keepdims=True)
        - scaled * jnp.mean(weighted * scaled, axis=-1, keepdims=True)
    )
    return (inverse * inner_term, jnp.sum(upstream * scaled, axis=0), jnp.sum(upstream, axis=0))


def gelu_slope(values):
    return 0.5 * (1.0 + lax.erf(values * ROOT_HALF)) + values * INV_ROOT_TWOPI * jnp.exp(
        -0.5 * values * values
    )


def masked_scores(query_seq, key_seq, label_seq):
    scores = jnp.einsum(
        "qhe,khe->hqk", query_seq, key_seq, preferred_element_type=jnp.float32
    ) * HEAD_DIM ** (-0.5)
    allowed = label_seq[:, None] == label_seq[None, :]
    return jnp.where(allowed[None], scores, MASKED)


def attend(queries, key_rows, value_rows, labels):
    row_count, local_width = queries.shape
    heads_here = local_width // HEAD_DIM
    shaped = [
        member.reshape(1, row_count, heads_here, HEAD_DIM)
        for member in (queries, key_rows, value_rows)
    ]

    def one_sequence(pieces):
        query_seq, key_seq, value_seq, label_seq = pieces
        scores = masked_scores(query_seq, key_seq, label_seq)
        largest = jnp.max(scores, axis=-1, keepdims=True)
        total_mass = jnp.sum(jnp.exp(scores - largest), axis=-1, keepdims=True)
        log_total = largest + jnp.log(total_mass)
        weights = jnp.exp(scores - log_total).astype(jnp.bfloat16)
        context = jnp.einsum("hqk,khe->qhe", weights, value_seq, preferred_element_type=jnp.float32)
        return (context.astype(jnp.bfloat16), log_total[..., 0])

    context, log_total = lax.map(
        one_sequence, (shaped[0], shaped[1], shaped[2], labels.reshape(1, row_count))
    )
    return (context.reshape(row_count, local_width), log_total)


def attend_back(queries, key_rows, value_rows, labels, log_total, grad_context):
    row_count, local_width = queries.shape
    heads_here = local_width // HEAD_DIM
    shaped = [
        member.reshape(1, row_count, heads_here, HEAD_DIM)
        for member in (queries, key_rows, value_rows, grad_context)
    ]
    score_scale = HEAD_DIM ** (-0.5)

    def one_sequence(pieces):
        query_seq, key_seq, value_seq, label_seq, total_seq, grad_seq = pieces
        scores = masked_scores(query_seq, key_seq, label_seq)
        weights = jnp.exp(scores - total_seq[..., None])
        weights_low = weights.astype(jnp.bfloat16)
        grad_weights = jnp.einsum(
            "qhe,khe->hqk", grad_seq, value_seq, preferred_element_type=jnp.float32
        )
        inner_term = jnp.sum(weights * grad_weights, axis=-1, keepdims=True)
        grad_scores = (weights * (grad_weights - inner_term)).astype(jnp.bfloat16)
        grad_query = (
            jnp.einsum("hqk,khe->qhe", grad_scores, key_seq, preferred_element_type=jnp.float32)
            * score_scale
        )
        grad_keys = (
            jnp.einsum("hqk,qhe->khe", grad_scores, query_seq, preferred_element_type=jnp.float32)
            * score_scale
        )
        grad_values = jnp.einsum(
            "hqk,qhe->khe", weights_low, grad_seq, preferred_element_type=jnp.float32
        )
        return jnp.stack((grad_query, grad_keys, grad_values), axis=1).astype(jnp.bfloat16)

    stacked = lax.map(
        one_sequence,
        (shaped[0], shaped[1], shaped[2], labels.reshape(1, row_count), log_total, shaped[3]),
    )
    return stacked.reshape(row_count, 3, local_width)


def layer_forward(current, labels, weights, vectors):
    w_qkv, w_o, w_in, w_out = weights
    gains, biases, query_bias, value_bias, local_hidden_bias = vectors
    gathered = lax.all_gather(current, "tensor", axis=0, tiled=True)
    projected = jnp.einsum("gd,dcn->gcn", gathered, w_qkv, preferred_element_type=jnp.float32)
    queries = (projected[:, 0] + query_bias).astype(jnp.bfloat16)
    key_rows = projected[:, 1].astype(jnp.bfloat16)
    value_rows = (projected[:, 2] + value_bias).astype(jnp.bfloat16)
    context, log_total = attend(queries, key_rows, value_rows, labels)
    partial_value = jnp.dot(context, w_o, preferred_element_type=jnp.float32)
    mixed_rows = lax.psum_scatter(partial_value, "tensor", scatter_dimension=0, tiled=True)
    normed, scaled_one, inverse_one = norm_forward(
        current.astype(jnp.float32) + mixed_rows + biases[2], gains[0], biases[3]
    )
    spread_rows = lax.all_gather(normed.astype(jnp.bfloat16), "tensor", axis=0, tiled=True)
    hidden = jnp.dot(spread_rows, w_in, preferred_element_type=jnp.float32) + local_hidden_bias
    active = jax.nn.gelu(hidden, approximate=False).astype(jnp.bfloat16)
    partial_out = jnp.dot(active, w_out, preferred_element_type=jnp.float32)
    branch = lax.psum_scatter(
        partial_out.astype(jnp.bfloat16), "tensor", scatter_dimension=0, tiled=True
    ).astype(jnp.float32)
    final_rows, scaled_two, inverse_two = norm_forward(
        normed + branch + biases[4], gains[1], biases[5]
    )
    kept_state = (
        gathered,
        queries,
        key_rows,
        value_rows,
        context,
        log_total,
        scaled_one,
        inverse_one,
        spread_rows,
        hidden,
        active,
        scaled_two,
        inverse_two,
    )
    return (final_rows.astype(jnp.bfloat16), kept_state)


def layer_backward(upstream, kept_state, labels, weights, gains):
    (
        gathered,
        queries,
        key_rows,
        value_rows,
        context,
        log_total,
        scaled_one,
        inverse_one,
        spread_rows,
        hidden,
        active,
        scaled_two,
        inverse_two,
    ) = kept_state
    w_qkv, w_o, w_in, w_out = weights
    grad_second, gain_two, shift_two = norm_backward(upstream, scaled_two, inverse_two, gains[1])
    grad_feed = lax.all_gather(grad_second.astype(jnp.bfloat16), "tensor", axis=0, tiled=True)
    grad_active = dot_cols(grad_feed, w_out)
    grad_w_out = dot_rows(active, grad_feed)
    grad_hidden = (grad_active * gelu_slope(hidden)).astype(jnp.bfloat16)
    grad_w_in = dot_rows(spread_rows, grad_hidden)
    grad_spread = dot_cols(grad_hidden, w_in)
    grad_normed = grad_second + lax.psum_scatter(
        grad_spread.astype(jnp.bfloat16), "tensor", scatter_dimension=0, tiled=True
    ).astype(jnp.float32)
    grad_first, gain_one, shift_one = norm_backward(grad_normed, scaled_one, inverse_one, gains[0])
    grad_mix = lax.all_gather(grad_first.astype(jnp.bfloat16), "tensor", axis=0, tiled=True)
    grad_context = dot_cols(grad_mix, w_o).astype(jnp.bfloat16)
    grad_w_o = dot_rows(context, grad_mix)
    grad_project = attend_back(queries, key_rows, value_rows, labels, log_total, grad_context)
    grad_w_qkv = jnp.einsum(
        "gd,gcn->dcn", gathered, grad_project, preferred_element_type=jnp.float32
    )
    grad_gathered = jnp.einsum(
        "gcn,dcn->gd", grad_project, w_qkv, preferred_element_type=jnp.float32
    )
    grad_current = grad_first + lax.psum_scatter(
        grad_gathered.astype(jnp.bfloat16), "tensor", scatter_dimension=0, tiled=True
    ).astype(jnp.float32)
    column_sums = jnp.sum(grad_project.astype(jnp.float32), axis=0)
    gain_grads = jnp.stack([gain_one, gain_two])
    row_grads = jnp.stack(
        [jnp.sum(grad_first, axis=0), shift_one, jnp.sum(grad_second, axis=0), shift_two]
    )
    local_grads = jnp.stack([column_sums[0], column_sums[2]])
    hidden_grads = jnp.sum(grad_hidden.astype(jnp.float32), axis=0)
    return (
        grad_current,
        (grad_w_qkv, grad_w_o, grad_w_in, grad_w_out),
        (gain_grads, row_grads, local_grads, hidden_grads),
    )


def body(inputs, segments, cotangent, w_qkv, w_o, w_in, w_out, ln_gains, model_biases, hidden_bias):
    section_first = lax.axis_index("pipe") == 0
    column = lax.axis_index("tensor")
    micro_count = inputs.shape[0]
    row_count = inputs.shape[1]
    model_width = model_biases.shape[-1]
    hidden_width = hidden_bias.shape[-1]
    width_local = w_qkv.shape[-1]
    hidden_local = w_in.shape[-1]
    gains = ln_gains[0]
    biases = model_biases[0]
    query_bias = lax.dynamic_slice_in_dim(biases[0], column * width_local, width_local)
    value_bias = lax.dynamic_slice_in_dim(biases[1], column * width_local, width_local)
    local_hidden_bias = lax.dynamic_slice_in_dim(
        hidden_bias[0], column * hidden_local, hidden_local
    )
    vectors = (gains, biases, query_bias, value_bias, local_hidden_bias)
    shards = (w_qkv[0], w_o[0], w_in[0], w_out[0])
    blank_rows = jnp.zeros((row_count, model_width), jnp.bfloat16)
    incoming = blank_rows
    returning = blank_rows
    kept_list = []
    forward_list = []
    backward_list = []
    weight_totals = None
    vector_totals = None
    for tick_index in range(micro_count + 2):
        weights = (
            lax.all_gather(shards[0], "dp", axis=0, tiled=True),
            lax.all_gather(shards[1], "dp", axis=1, tiled=True),
            lax.all_gather(shards[2], "dp", axis=0, tiled=True),
            lax.all_gather(shards[3], "dp", axis=1, tiled=True),
        )
        own_rows = inputs[tick_index] if tick_index < micro_count else blank_rows
        current = jnp.where(section_first, own_rows, incoming)
        labels_forward = jnp.where(
            section_first,
            segments[min(tick_index, micro_count - 1)],
            segments[max(min(tick_index - 1, micro_count - 1), 0)],
        )
        final_rows, kept_state = layer_forward(current, labels_forward, weights, vectors)
        forward_list.append(final_rows)
        incoming = shifted(final_rows, "pipe", 1)
        given_grad = cotangent[tick_index - 1] if 1 <= tick_index <= micro_count else blank_rows
        upstream = jnp.where(section_first, returning, given_grad).astype(jnp.float32)
        earlier = kept_list[tick_index - 2] if tick_index >= 2 else kept_state
        chosen_state = jax.tree.map(
            lambda first_item, second_item: jnp.where(section_first, first_item, second_item),
            earlier,
            kept_state,
        )
        labels_backward = jnp.where(
            section_first,
            segments[max(min(tick_index - 2, micro_count - 1), 0)],
            segments[max(min(tick_index - 1, micro_count - 1), 0)],
        )
        grad_current, weight_grads, vector_grads = layer_backward(
            upstream, chosen_state, labels_backward, weights, gains
        )
        if tick_index == 0:
            weight_totals = weight_grads
            vector_totals = vector_grads
        else:
            weight_totals = jax.tree.map(jnp.add, weight_totals, weight_grads)
            vector_totals = jax.tree.map(jnp.add, vector_totals, vector_grads)
        grad_low = grad_current.astype(jnp.bfloat16)
        backward_list.append(grad_low)
        returning = shifted(grad_low, "pipe", -1)
        kept_list.append(kept_state)
    summed = (
        lax.psum_scatter(
            weight_totals[0].astype(jnp.bfloat16), "dp", scatter_dimension=0, tiled=True
        ).astype(jnp.float32),
        lax.psum_scatter(
            weight_totals[1].astype(jnp.bfloat16), "dp", scatter_dimension=1, tiled=True
        ).astype(jnp.float32),
        lax.psum_scatter(
            weight_totals[2].astype(jnp.bfloat16), "dp", scatter_dimension=0, tiled=True
        ).astype(jnp.float32),
        lax.psum_scatter(
            weight_totals[3].astype(jnp.bfloat16), "dp", scatter_dimension=1, tiled=True
        ).astype(jnp.float32),
    )
    gain_grads, row_grads, local_grads, hidden_grads = vector_totals
    zero_index = jnp.zeros((), jnp.int32)
    placed = lax.dynamic_update_slice(
        jnp.zeros((2, model_width), jnp.float32), local_grads, (zero_index, column * width_local)
    )
    bias_full = jnp.concatenate([placed, row_grads], axis=0)
    hidden_full = lax.dynamic_update_slice(
        jnp.zeros((hidden_width,), jnp.float32), hidden_grads, (column * hidden_local,)
    )
    vector_sums = (
        lax.psum_scatter(gain_grads, ("dp", "tensor"), scatter_dimension=1, tiled=True),
        lax.psum_scatter(bias_full, ("dp", "tensor"), scatter_dimension=1, tiled=True),
        lax.psum_scatter(hidden_full, ("dp", "tensor"), scatter_dimension=0, tiled=True),
    )
    section_rows = jnp.stack(
        [
            jnp.where(section_first, forward_list[batch_index], forward_list[batch_index + 1])
            for batch_index in range(micro_count)
        ]
    )[None]
    grad_rows = jnp.stack(
        [
            jnp.where(section_first, backward_list[batch_index + 2], backward_list[batch_index + 1])
            for batch_index in range(micro_count)
        ]
    )[None]
    return (
        section_rows,
        grad_rows,
        summed[0][None],
        summed[1][None],
        summed[2][None],
        summed[3][None],
        vector_sums[0][None],
        vector_sums[1][None],
        vector_sums[2][None],
    )


def solution(mesh):
    return jax.shard_map(
        body,
        mesh=mesh,
        in_specs=(
            P(None, ("dp", "tensor"), None),
            P(None, "dp"),
            P(None, ("dp", "tensor"), None),
            P("pipe", "dp", None, "tensor"),
            P("pipe", "tensor", "dp"),
            P("pipe", "dp", "tensor"),
            P("pipe", "tensor", "dp"),
            P("pipe", None, None),
            P("pipe", None, None),
            P("pipe", None),
        ),
        out_specs=(
            P("pipe", None, ("dp", "tensor"), None),
            P("pipe", None, ("dp", "tensor"), None),
            P("pipe", "dp", None, "tensor"),
            P("pipe", "tensor", "dp"),
            P("pipe", "dp", "tensor"),
            P("pipe", "tensor", "dp"),
            P("pipe", None, ("dp", "tensor")),
            P("pipe", None, ("dp", "tensor")),
            P("pipe", ("dp", "tensor")),
        ),
        check_vma=False,
    )
```

profile of v0, /device:TPU:0, one launch (start us, length us, event | category | flops | bytes accessed | tf_op | source)
XLA Modules:
  0.0 1324.4 jit_solution(16337392418680728141)
XLA Ops:
  43.2 27.1 %reduce-scatter.35.cloned.1.call-done = f32[64,1024]{1,0:T(8,128)} async-done(((f32[256,1024]{1,0:T(8,128)}), f32[64,1024]{1,0:T(8,128)}) %reduce-scatter.35.cloned.1.call-update) | async-done | bytes 262160 | tf_op jit(solution)/shard_map/reduce_scatter | solution.py:136
  98.4 18.8 %all-gather.13.cloned.1.call-done = bf16[1,1024,1024]{2,1,0:T(8,128)(2,1)} async-done(((bf16[1,1024,256]{2,1,0:T(8,128)(2,1)}), bf16[1,1024,1024]{2,1,0:T(8,128)(2,1)}) %all-gather.13.cloned.1.call-update) | async-done | bytes 2097168 | tf_op jit(solution)/shard_map/all_gather | solution.py:254
  121.6 20.6 %reduce-scatter.37.cloned.1.call-done = bf16[64,1024]{1,0:T(8,128)(2,1)} async-done(((bf16[256,1024]{1,0:T(8,128)(2,1)}), bf16[64,1024]{1,0:T(8,128)(2,1)}) %reduce-scatter.37.cloned.1.call-update) | async-done | bytes 131088 | tf_op jit(solution)/shard_map/reduce_scatter | solution.py:144
  167.5 19.8 %reduce-scatter.55.cloned.1.call-done = bf16[64,1024]{1,0:T(8,128)(2,1)} async-done(((bf16[256,1024]{1,0:T(8,128)(2,1)}), bf16[64,1024]{1,0:T(8,128)(2,1)}) %reduce-scatter.55.cloned.1.call-update) | async-done | bytes 131088 | tf_op jit(solution)/shard_map/reduce_scatter | solution.py:192
  218.4 25.7 %reduce-scatter.39.cloned.1.call-done = f32[64,1024]{1,0:T(8,128)} async-done(((f32[256,1024]{1,0:T(8,128)}), f32[64,1024]{1,0:T(8,128)}) %reduce-scatter.39.cloned.1.call-update) | async-done | bytes 262160 | tf_op jit(solution)/shard_map/reduce_scatter | solution.py:136
  399.1 26.2 %reduce-scatter.43.cloned.1.call-done = f32[64,1024]{1,0:T(8,128)} async-done(((f32[256,1024]{1,0:T(8,128)}), f32[64,1024]{1,0:T(8,128)}) %reduce-scatter.43.cloned.1.call-update) | async-done | bytes 262160 | tf_op jit(solution)/shard_map/reduce_scatter | solution.py:136
  452.7 18.0 %all_gather.121 = bf16[256,1024]{1,0:T(8,128)(2,1)S(1)} all-gather(bf16[64,1024]{1,0:T(8,128)(2,1)S(1)} %convert_element_type.649), channel_id=1, replica_groups=mesh['pipe'=2,'dp'=4,'tensor'=4] {'tensor'}, dimensions={0}, use_global_device_ids=true | all-gather | bytes 655360 | tf_op jit(solution)/shard_map/all_gather | solution.py:196
  490.1 17.9 %all_gather.114 = bf16[256,1024]{1,0:T(8,128)(2,1)S(1)} all-gather(bf16[64,1024]{1,0:T(8,128)(2,1)S(1)} %bitcast_select_fusion.6), channel_id=1, replica_groups=mesh['pipe'=2,'dp'=4,'tensor'=4] {'tensor'}, dimensions={0}, use_global_device_ids=true | all-gather | bytes 655360 | tf_op jit(solution)/shard_map/all_gather | solution.py:129
  523.9 20.3 %all_gather.122 = bf16[256,1024]{1,0:T(8,128)(2,1)S(1)} all-gather(bf16[64,1024]{1,0:T(8,128)(2,1)S(1)} %get-tuple-element.384), channel_id=1, replica_groups=mesh['pipe'=2,'dp'=4,'tensor'=4] {'tensor'}, dimensions={0}, use_global_device_ids=true | all-gather | bytes 655360 | tf_op jit(solution)/shard_map/all_gather | solution.py:186
  551.2 20.7 %reduce-scatter.63.cloned.1.call-done = bf16[64,1024]{1,0:T(8,128)(2,1)} async-done(((bf16[256,1024]{1,0:T(8,128)(2,1)}), bf16[64,1024]{1,0:T(8,128)(2,1)}) %reduce-scatter.63.cloned.1.call-update) | async-done | bytes 131088 | tf_op jit(solution)/shard_map/reduce_scatter | solution.py:192
  596.4 20.2 %reduce-scatter.49.cloned.1.call-done = bf16[64,1024]{1,0:T(8,128)(2,1)} async-done(((bf16[256,1024]{1,0:T(8,128)(2,1)}), bf16[64,1024]{1,0:T(8,128)(2,1)}) %reduce-scatter.49.cloned.1.call-update) | async-done | bytes 131088 | tf_op jit(solution)/shard_map/reduce_scatter | solution.py:144
  645.1 27.3 %reduce-scatter.51.cloned.1.call-done = f32[64,1024]{1,0:T(8,128)} async-done(((f32[256,1024]{1,0:T(8,128)}), f32[64,1024]{1,0:T(8,128)}) %reduce-scatter.51.cloned.1.call-update) | async-done | bytes 262160 | tf_op jit(solution)/shard_map/reduce_scatter | solution.py:136
  698.4 18.1 %all_gather.123 = bf16[256,1024]{1,0:T(8,128)(2,1)S(1)} all-gather(bf16[64,1024]{1,0:T(8,128)(2,1)S(1)} %convert_element_type.661), channel_id=1, replica_groups=mesh['pipe'=2,'dp'=4,'tensor'=4] {'tensor'}, dimensions={0}, use_global_device_ids=true | all-gather | bytes 655360 | tf_op jit(solution)/shard_map/all_gather | solution.py:196
  736.3 17.8 %all_gather.128 = bf16[256,1024]{1,0:T(8,128)(2,1)S(1)} all-gather(bf16[64,1024]{1,0:T(8,128)(2,1)S(1)} %broadcast_select_fusion.9), channel_id=1, replica_groups=mesh['pipe'=2,'dp'=4,'tensor'=4] {'tensor'}, dimensions={0}, use_global_device_ids=true | all-gather | bytes 655360 | tf_op jit(solution)/shard_map/all_gather | solution.py:129
  769.7 21.1 %all_gather.124 = bf16[256,1024]{1,0:T(8,128)(2,1)S(1)} all-gather(bf16[64,1024]{1,0:T(8,128)(2,1)S(1)} %get-tuple-element.377), channel_id=1, replica_groups=mesh['pipe'=2,'dp'=4,'tensor'=4] {'tensor'}, dimensions={0}, use_global_device_ids=true | all-gather | bytes 655360 | tf_op jit(solution)/shard_map/all_gather | solution.py:186
  798.7 19.1 %reduce-scatter.67.cloned.1.call-done = bf16[64,1024]{1,0:T(8,128)(2,1)} async-done(((bf16[256,1024]{1,0:T(8,128)(2,1)}), bf16[64,1024]{1,0:T(8,128)(2,1)}) %reduce-scatter.67.cloned.1.call-update) | async-done | bytes 131088 | tf_op jit(solution)/shard_map/reduce_scatter | solution.py:192
  847.5 18.1 %all_gather.129 = bf16[256,1024]{1,0:T(8,128)(2,1)S(1)} all-gather(bf16[64,1024]{1,0:T(8,128)(2,1)} %get-tuple-element.464), channel_id=1, replica_groups=mesh['pipe'=2,'dp'=4,'tensor'=4] {'tensor'}, dimensions={0}, use_global_device_ids=true | all-gather | bytes 655360 | tf_op jit(solution)/shard_map/all_gather | solution.py:140
  881.6 20.7 %all_gather.126 = bf16[256,1024]{1,0:T(8,128)(2,1)S(1)} all-gather(bf16[64,1024]{1,0:T(8,128)(2,1)S(1)} %get-tuple-element.370), channel_id=1, replica_groups=mesh['pipe'=2,'dp'=4,'tensor'=4] {'tensor'}, dimensions={0}, use_global_device_ids=true | all-gather | bytes 655360 | tf_op jit(solution)/shard_map/all_gather | solution.py:186
  1102.5 58.1 %all-reduce = f32[4096]{0:T(1024)S(1)} all-reduce(f32[4096]{0:T(1024)S(1)} %add_dynamic-update-slice_fusion), channel_id=37, replica_groups=mesh['pipe'=2,'dp'=4,'tensor'=4] {'dp','tensor'}, use_global_device_ids=true, to_apply=%region_143.144.clone | all-reduce | flops 4096 | bytes 32768
  1172.3 22.4 %reduce-scatter.81.cloned.1.call-done = bf16[64,1024]{1,0:T(8,128)(2,1)} async-done(((bf16[256,1024]{1,0:T(8,128)(2,1)}), bf16[64,1024]{1,0:T(8,128)(2,1)}) %reduce-scatter.81.cloned.1.call-update) | async-done | bytes 131088 | tf_op jit(solution)/shard_map/reduce_scatter | solution.py:206
  1196.5 21.0 %reduce-scatter.85.cloned.1.call-done = bf16[256,256]{1,0:T(8,128)(2,1)} async-done(((bf16[256,1024]{1,0:T(8,128)(2,1)}), bf16[256,256]{1,0:T(8,128)(2,1)}) %reduce-scatter.85.cloned.1.call-update) | async-done | bytes 131088 | tf_op jit(solution)/shard_map/reduce_scatter | solution.py:296
  1219.1 32.1 %reduce-scatter.87.cloned.1.call-done = bf16[256,1024]{1,0:T(8,128)(2,1)} async-done(((bf16[1024,1024]{1,0:T(8,128)(2,1)}), bf16[256,1024]{1,0:T(8,128)(2,1)}) %reduce-scatter.87.cloned.1.call-update) | async-done | bytes 524304 | tf_op jit(solution)/shard_map/reduce_scatter | solution.py:299
  1253.3 31.6 %reduce-scatter.89.cloned.1.call-done = bf16[1024,256]{1,0:T(8,128)(2,1)} async-done(((bf16[1024,1024]{1,0:T(8,128)(2,1)}), bf16[1024,256]{1,0:T(8,128)(2,1)}) %reduce-scatter.89.cloned.1.call-update) | async-done | bytes 524304 | tf_op jit(solution)/shard_map/reduce_scatter | solution.py:302
  1287.0 28.4 %reduce-scatter.83.cloned.1.call-done = bf16[256,3,256]{2,0,1:T(8,128)(2,1)} async-done(((bf16[1024,3,256]{2,0,1:T(8,128)(2,1)}), bf16[256,3,256]{2,0,1:T(8,128)(2,1)}) %reduce-scatter.83.cloned.1.call-update) | async-done | bytes 393232 | tf_op jit(solution)/shard_map/reduce_scatter | solution.py:293
  (1219 shorter events, 733.2 us)
Async XLA Ops:
  42.5 74.7 %all-gather.13.cloned.1.call-start = ((), (), s32[]{:S(2)}) async-start(), calls=%async_computation.60 | async-start | bytes 2621440 | tf_op jit(solution)/shard_map/all_gather | solution.py:254
  43.1 99.2 %reduce-scatter.37.cloned.1.call-start = ((), (), s32[]{:S(2)}) async-start(), calls=%async_computation.31 | async-start | bytes 655360 | tf_op jit(solution)/shard_map/reduce_scatter | solution.py:144
  120.3 66.9 %reduce-scatter.55.cloned.1.call-start = ((), (), s32[]{:S(2)}) async-start(), calls=%async_computation.40 | async-start | bytes 655360 | tf_op jit(solution)/shard_map/reduce_scatter | solution.py:192
  166.8 77.3 %reduce-scatter.39.cloned.1.call-start = ((), (), s32[]{:S(2)}) async-start(), calls=%async_computation.32 | async-start | bytes 1310720 | tf_op jit(solution)/shard_map/reduce_scatter | solution.py:136
  216.7 94.3 %reduce-scatter.41.cloned.1.call-start = ((), (), s32[]{:S(2)}) async-start(), calls=%async_computation.33 | async-start | bytes 655360 | tf_op jit(solution)/shard_map/reduce_scatter | solution.py:144
  297.9 99.6 %reduce-scatter.59.cloned.1.call-start = ((), (), s32[]{:S(2)}) async-start(), calls=%async_computation.42 | async-start | bytes 655360 | tf_op jit(solution)/shard_map/reduce_scatter | solution.py:192
  383.9 95.0 %reduce-scatter.45.cloned.1.call-start = ((), (), s32[]{:S(2)}) async-start(), calls=%async_computation.35 | async-start | bytes 655360 | tf_op jit(solution)/shard_map/reduce_scatter | solution.py:144
  451.6 61.8 %reduce-scatter.61.cloned.1.call-start = ((), (), s32[]{:S(2)}) async-start(), calls=%async_computation.43 | async-start | bytes 655360 | tf_op jit(solution)/shard_map/reduce_scatter | solution.py:206
  488.1 61.8 %reduce-scatter.47.cloned.1.call-start = ((), (), s32[]{:S(2)}) async-start(), calls=%async_computation.36 | async-start | bytes 1310720 | tf_op jit(solution)/shard_map/reduce_scatter | solution.py:136
  549.8 66.8 %reduce-scatter.49.cloned.1.call-start = ((), (), s32[]{:S(2)}) async-start(), calls=%async_computation.37 | async-start | bytes 655360 | tf_op jit(solution)/shard_map/reduce_scatter | solution.py:144
  596.1 76.3 %reduce-scatter.51.cloned.1.call-start = ((), (), s32[]{:S(2)}) async-start(), calls=%async_computation.38 | async-start | bytes 1310720 | tf_op jit(solution)/shard_map/reduce_scatter | solution.py:136
  645.0 82.0 %reduce-scatter.53.cloned.1.call-start = ((), (), s32[]{:S(2)}) async-start(), calls=%async_computation.39 | async-start | bytes 655360 | tf_op jit(solution)/shard_map/reduce_scatter | solution.py:144
  734.6 61.5 %reduce-scatter.75.cloned.1.call-start = ((), (), s32[]{:S(2)}) async-start(), calls=%async_computation.50 | async-start | bytes 1310720 | tf_op jit(solution)/shard_map/reduce_scatter | solution.py:136
  794.2 75.0 %reduce-scatter.69.cloned.1.call-start = ((), (), s32[]{:S(2)}) async-start(), calls=%async_computation.47 | async-start | bytes 655360 | tf_op jit(solution)/shard_map/reduce_scatter | solution.py:206
  846.8 71.2 %reduce-scatter.77.cloned.1.call-start = ((), (), s32[]{:S(2)}) async-start(), calls=%async_computation.51 | async-start | bytes 655360 | tf_op jit(solution)/shard_map/reduce_scatter | solution.py:144
  908.5 74.3 %reduce-scatter.73.cloned.1.call-start = ((), (), s32[]{:S(2)}) async-start(), calls=%async_computation.49 | async-start | bytes 655360 | tf_op jit(solution)/shard_map/reduce_scatter | solution.py:206
  962.4 71.3 %reduce-scatter.79.cloned.1.call-start = ((), (), s32[]{:S(2)}) async-start(), calls=%async_computation.52 | async-start | bytes 655360 | tf_op jit(solution)/shard_map/reduce_scatter | solution.py:192
  1013.7 147.5 %reduce-scatter.91.cloned.1.call-start = ((), (), s32[]{:S(2)}) async-start(), calls=%async_computation.61 | async-start | bytes 557056
  1057.3 113.6 %reduce-scatter.93.cloned.1.call-start = ((), (), s32[]{:S(2)}) async-start(), calls=%async_computation.62 | async-start | bytes 557056
  1060.2 134.4 %reduce-scatter.81.cloned.1.call-start = ((), (), s32[]{:S(2)}) async-start(), calls=%async_computation.53 | async-start | bytes 655360 | tf_op jit(solution)/shard_map/reduce_scatter | solution.py:206
  1062.8 154.7 %reduce-scatter.85.cloned.1.call-start = ((), (), s32[]{:S(2)}) async-start(), calls=%async_computation.55 | async-start | bytes 655360 | tf_op jit(solution)/shard_map/reduce_scatter | solution.py:296
  1069.9 181.3 %reduce-scatter.87.cloned.1.call-start = ((), (), s32[]{:S(2)}) async-start(), calls=%async_computation.56 | async-start | bytes 2621440 | tf_op jit(solution)/shard_map/reduce_scatter | solution.py:299
  1080.0 204.9 %reduce-scatter.89.cloned.1.call-start = ((), (), s32[]{:S(2)}) async-start(), calls=%async_computation.57 | async-start | bytes 2621440 | tf_op jit(solution)/shard_map/reduce_scatter | solution.py:302
  1091.6 223.8 %reduce-scatter.83.cloned.1.call-start = ((), (), s32[]{:S(2)}) async-start(), calls=%async_computation.54 | async-start | bytes 1966080 | tf_op jit(solution)/shard_map/reduce_scatter | solution.py:293
  (400 other events, 4967.2 us)
Sparse Core Ops, SparseCore 0:
  10.1 22.6 all-gather.8
  41.9 28.3 reduce-scatter.34
  71.8 21.0 all-gather.10
  94.3 22.8 all-gather.12
  120.4 21.8 reduce-scatter.36
  216.8 27.2 reduce-scatter.38
  376.9 20.5 reduce-scatter.58
  399.8 25.5 reduce-scatter.42
  451.7 22.2 reduce-scatter.44
  488.2 21.2 reduce-scatter.60
  513.5 35.2 reduce-scatter.46
  645.2 27.2 reduce-scatter.50
  698.4 21.8 reduce-scatter.52
  734.7 21.0 reduce-scatter.64
  758.6 35.9 reduce-scatter.74
  846.9 22.0 reduce-scatter.68
  877.9 25.8 reduce-scatter.76
  908.6 22.3 reduce-scatter.70
  1057.4 54.6 reduce-scatter.90
  1115.6 55.2 reduce-scatter.92
  1173.7 20.8 reduce-scatter.80
  1220.0 31.1 reduce-scatter.86
  1253.7 31.1 reduce-scatter.88
  1287.3 28.0 reduce-scatter.82
  (9 shorter events, 181.0 us)
where the time goes:
time: 1340 us; the launch traced here: 1320 us
  waiting for transfers between devices  477 us (36%)
  blocking collectives  467 us (35%)
  matrix products  163 us (12%)
  other arithmetic  113 us (8%)
  local copies, waits for them, and re-layouts  58.1 us (4%)
  starting transfers between devices  25.9 us (2%)
  between operations  20.3 us (2%)
    all_gather x6, blocking collectives, layer_backward(): lax.all_gather(grad_second.astype(jnp.bfloat16), 'tensor', axis=0, tiled=...  108 us
    reduce_scatter x6, waiting for transfers between devices, layer_forward(): lax.psum_scatter(partial_value, 'tensor', scatter_dimension=0, tiled=True)  106 us
    reduce_scatter x6, waiting for transfers between devices, layer_backward(): lax.psum_scatter(grad_spread.astype(jnp.bfloat16), 'tensor', scatter_dime...  98.7 us
    all_gather x6, blocking collectives, layer_backward(): lax.all_gather(grad_first.astype(jnp.bfloat16), 'tensor', axis=0, tiled=T...  98.5 us
    all_gather x6, blocking collectives, layer_forward(): gathered = lax.all_gather(current, 'tensor', axis=0, tiled=True)  97.8 us
    all_gather x6, blocking collectives, layer_forward(): lax.all_gather(normed.astype(jnp.bfloat16), 'tensor', axis=0, tiled=True)  97 us
    unnamed x1, blocking collectives  58.1 us
    reduce_scatter x6, waiting for transfers between devices, layer_forward(): lax.psum_scatter(partial_out.astype(jnp.bfloat16), 'tensor', scatter_dime...  54 us
  transfers between devices with their start and end apart: 43, of which 31 were waited for; matrix products, arithmetic and copies ran while one was open for 13% of the time, Pallas kernels for 0%

commit v1 on v0

--- a/solution.py
+++ b/solution.py
@@ -8,6 +8,27 @@
 MASKED = -1000000000.0
 ROOT_HALF = 0.7071067811865476
 INV_ROOT_TWOPI = 0.3989422804014327
+
+
+def ring_gather(x, axis, dim):
+    count, index, rows = (lax.axis_size(axis), lax.axis_index(axis), x.shape[dim])
+    right = [(i, (i + 1) % count) for i in range(count)]
+    behind = [(i, (i - 1) % count) for i in range(count)]
+    out = jnp.zeros((*x.shape[:dim], count * rows, *x.shape[dim + 1 :]), x.dtype)
+    out = lax.dynamic_update_slice_in_dim(out, x, index * rows, axis=dim)
+    from_left = from_right = x
+    middle = count // 2
+    for turn in range(1, middle + 1):
+        from_left = lax.ppermute(from_left, axis, right)
+        out = lax.dynamic_update_slice_in_dim(
+            out, from_left, (index - turn) % count * rows, axis=dim
+        )
+        if turn < count - middle:
+            from_right = lax.ppermute(from_right, axis, behind)
+            out = lax.dynamic_update_slice_in_dim(
+                out, from_right, (index + turn) % count * rows, axis=dim
+            )
+    return out
 
 
 def shifted(block, axis, distance):
@@ -126,7 +147,7 @@
 def layer_forward(current, labels, weights, vectors):
     w_qkv, w_o, w_in, w_out = weights
     gains, biases, query_bias, value_bias, local_hidden_bias = vectors
-    gathered = lax.all_gather(current, "tensor", axis=0, tiled=True)
+    gathered = ring_gather(current, "tensor", 0)
     projected = jnp.einsum("gd,dcn->gcn", gathered, w_qkv, preferred_element_type=jnp.float32)
     queries = (projected[:, 0] + query_bias).astype(jnp.bfloat16)
     key_rows = projected[:, 1].astype(jnp.bfloat16)

time: 1340 us -> 1320 us (0.985)
  blocking collectives: 467 us -> 371 us
  waiting for transfers between devices: 477 us -> 534 us
  starting transfers between devices: 25.9 us -> 51.8 us
    all_gather x6 -> x0, blocking collectives: 97.8 us -> none  [layer_forward(): gathered = lax.all_gather(current, 'tensor', axis=0, tiled=True)]
    ppermute x0 -> x18, waiting for transfers between devices: none -> 44.7 us  [the longest x12 44.7 us: ring_gather(): from_left = lax.ppermute(from_left, axis, right)]
    ppermute x0 -> x18, starting transfers between devices: none -> 24.9 us  [the longest x6 21.2 us: ring_gather(): from_right = lax.ppermute(from_right, axis, behind)]
    reduce_scatter x6, waiting for transfers between devices: 51.7 us -> 68.2 us  [layer_backward(): lax.psum_scatter(grad_gathered.astype(jnp.bfloat16), 'tensor', scatter_di...]
    unnamed x770 -> x836, local copies, waits for them, and re-layouts: 39.2 us -> 39.3 us
  transfers between devices with their start and end apart: 43 -> 61, of which waited for: 31 -> 45; matrix products, arithmetic and copies ran while one was open for 13% -> 14% of each run, Pallas kernels for 0% -> 0%
where the time goes in v1:
time: 1320 us; the launch traced here: 1310 us
  waiting for transfers between devices  534 us (40%)
  blocking collectives  371 us (28%)
  matrix products  161 us (12%)
  other arithmetic  110 us (8%)
  local copies, waits for them, and re-layouts  62.5 us (5%)
  starting transfers between devices  51.8 us (4%)
  between operations  21 us (2%)
    all_gather x6, blocking collectives, layer_backward(): lax.all_gather(grad_second.astype(jnp.bfloat16), 'tensor', axis=0, tiled=...  108 us
    reduce_scatter x6, waiting for transfers between devices, layer_forward(): lax.psum_scatter(partial_value, 'tensor', scatter_dimension=0, tiled=True)  101 us
    all_gather x6, blocking collectives, layer_backward(): lax.all_gather(grad_first.astype(jnp.bfloat16), 'tensor', axis=0, tiled=T...  98.8 us
    reduce_scatter x6, waiting for transfers between devices, layer_backward(): lax.psum_scatter(grad_spread.astype(jnp.bfloat16), 'tensor', scatter_dime...  97.7 us
    all_gather x6, blocking collectives, layer_forward(): lax.all_gather(normed.astype(jnp.bfloat16), 'tensor', axis=0, tiled=True)  97.2 us
    reduce_scatter x6, waiting for transfers between devices, layer_backward(): lax.psum_scatter(grad_gathered.astype(jnp.bfloat16), 'tensor', scatter_di...  68.2 us
    unnamed x1, blocking collectives  58.2 us
    reduce_scatter x6, waiting for transfers between devices, layer_forward(): lax.psum_scatter(partial_out.astype(jnp.bfloat16), 'tensor', scatter_dime...  54.1 us
  transfers between devices with their start and end apart: 61, of which 45 were waited for; matrix products, arithmetic and copies ran while one was open for 14% of the time, Pallas kernels for 0%

profile of v1, /device:TPU:0, one launch (start us, length us, event | category | flops | bytes accessed | tf_op | source)
XLA Modules:
  0.0 1310.7 jit_solution(2642033085589980787)
XLA Ops:
  39.5 25.3 %reduce-scatter.35.cloned.1.call-done = f32[64,1024]{1,0:T(8,128)} async-done(((f32[256,1024]{1,0:T(8,128)}), f32[64,1024]{1,0:T(8,128)}) %reduce-scatter.35.cloned.1.call-update) | async-done | bytes 262160 | tf_op jit(solution)/shard_map/reduce_scatter | solution.py:157
  92.9 18.8 %all-gather.12.cloned.1.call-done = bf16[1,1024,1024]{2,1,0:T(8,128)(2,1)} async-done(((bf16[1,1024,256]{2,1,0:T(8,128)(2,1)}), bf16[1,1024,1024]{2,1,0:T(8,128)(2,1)}) %all-gather.12.cloned.1.call-update) | async-done | bytes 2097168 | tf_op jit(solution)/shard_map/all_gather | solution.py:275
  116.1 20.7 %reduce-scatter.37.cloned.1.call-done = bf16[64,1024]{1,0:T(8,128)(2,1)} async-done(((bf16[256,1024]{1,0:T(8,128)(2,1)}), bf16[64,1024]{1,0:T(8,128)(2,1)}) %reduce-scatter.37.cloned.1.call-update) | async-done | bytes 131088 | tf_op jit(solution)/shard_map/reduce_scatter | solution.py:165
  161.3 20.4 %reduce-scatter.55.cloned.1.call-done = bf16[64,1024]{1,0:T(8,128)(2,1)} async-done(((bf16[256,1024]{1,0:T(8,128)(2,1)}), bf16[64,1024]{1,0:T(8,128)(2,1)}) %reduce-scatter.55.cloned.1.call-update) | async-done | bytes 131088 | tf_op jit(solution)/shard_map/reduce_scatter | solution.py:213
  212.2 25.3 %reduce-scatter.39.cloned.1.call-done = f32[64,1024]{1,0:T(8,128)} async-done(((f32[256,1024]{1,0:T(8,128)}), f32[64,1024]{1,0:T(8,128)}) %reduce-scatter.39.cloned.1.call-update) | async-done | bytes 262160 | tf_op jit(solution)/shard_map/reduce_scatter | solution.py:157
  242.9 16.1 %all_gather.96 = bf16[256,1024]{1,0:T(8,128)(2,1)S(1)} all-gather(bf16[64,1024]{1,0:T(8,128)(2,1)S(1)} %convert_element_type.638), channel_id=1, replica_groups=mesh['pipe'=2,'dp'=4,'tensor'=4] {'tensor'}, dimensions={0}, use_global_device_ids=true | all-gather | bytes 655360 | tf_op jit(solution)/shard_map/all_gather | solution.py:217
  311.2 16.4 %reduce-scatter.57.cloned.1.call-done = bf16[64,1024]{1,0:T(8,128)(2,1)} async-done(((bf16[256,1024]{1,0:T(8,128)(2,1)}), bf16[64,1024]{1,0:T(8,128)(2,1)}) %reduce-scatter.57.cloned.1.call-update) | async-done | bytes 131088 | tf_op jit(solution)/shard_map/reduce_scatter | solution.py:227
  380.2 26.3 %reduce-scatter.43.cloned.1.call-done = f32[64,1024]{1,0:T(8,128)} async-done(((f32[256,1024]{1,0:T(8,128)}), f32[64,1024]{1,0:T(8,128)}) %reduce-scatter.43.cloned.1.call-update) | async-done | bytes 262160 | tf_op jit(solution)/shard_map/reduce_scatter | solution.py:157
  434.0 17.9 %all_gather.98 = bf16[256,1024]{1,0:T(8,128)(2,1)S(1)} all-gather(bf16[64,1024]{1,0:T(8,128)(2,1)S(1)} %convert_element_type.649), channel_id=1, replica_groups=mesh['pipe'=2,'dp'=4,'tensor'=4] {'tensor'}, dimensions={0}, use_global_device_ids=true | all-gather | bytes 655360 | tf_op jit(solution)/shard_map/all_gather | solution.py:217
  508.9 21.1 %all_gather.99 = bf16[256,1024]{1,0:T(8,128)(2,1)S(1)} all-gather(bf16[64,1024]{1,0:T(8,128)(2,1)S(1)} %get-tuple-element.386), channel_id=1, replica_groups=mesh['pipe'=2,'dp'=4,'tensor'=4] {'tensor'}, dimensions={0}, use_global_device_ids=true | all-gather | bytes 655360 | tf_op jit(solution)/shard_map/all_gather | solution.py:207
  537.0 20.9 %reduce-scatter.63.cloned.1.call-done = bf16[64,1024]{1,0:T(8,128)(2,1)} async-done(((bf16[256,1024]{1,0:T(8,128)(2,1)}), bf16[64,1024]{1,0:T(8,128)(2,1)}) %reduce-scatter.63.cloned.1.call-update) | async-done | bytes 131088 | tf_op jit(solution)/shard_map/reduce_scatter | solution.py:213
  582.7 20.3 %reduce-scatter.49.cloned.1.call-done = bf16[64,1024]{1,0:T(8,128)(2,1)} async-done(((bf16[256,1024]{1,0:T(8,128)(2,1)}), bf16[64,1024]{1,0:T(8,128)(2,1)}) %reduce-scatter.49.cloned.1.call-update) | async-done | bytes 131088 | tf_op jit(solution)/shard_map/reduce_scatter | solution.py:165
  632.6 24.2 %reduce-scatter.51.cloned.1.call-done = f32[64,1024]{1,0:T(8,128)} async-done(((f32[256,1024]{1,0:T(8,128)}), f32[64,1024]{1,0:T(8,128)}) %reduce-scatter.51.cloned.1.call-update) | async-done | bytes 262160 | tf_op jit(solution)/shard_map/reduce_scatter | solution.py:157
  683.4 18.1 %all_gather.100 = bf16[256,1024]{1,0:T(8,128)(2,1)S(1)} all-gather(bf16[64,1024]{1,0:T(8,128)(2,1)S(1)} %convert_element_type.661), channel_id=1, replica_groups=mesh['pipe'=2,'dp'=4,'tensor'=4] {'tensor'}, dimensions={0}, use_global_device_ids=true | all-gather | bytes 655360 | tf_op jit(solution)/shard_map/all_gather | solution.py:217
  757.8 21.1 %all_gather.101 = bf16[256,1024]{1,0:T(8,128)(2,1)S(1)} all-gather(bf16[64,1024]{1,0:T(8,128)(2,1)S(1)} %get-tuple-element.379), channel_id=1, replica_groups=mesh['pipe'=2,'dp'=4,'tensor'=4] {'tensor'}, dimensions={0}, use_global_device_ids=true | all-gather | bytes 655360 | tf_op jit(solution)/shard_map/all_gather | solution.py:207
  785.9 20.8 %reduce-scatter.67.cloned.1.call-done = bf16[64,1024]{1,0:T(8,128)(2,1)} async-done(((bf16[256,1024]{1,0:T(8,128)(2,1)}), bf16[64,1024]{1,0:T(8,128)(2,1)}) %reduce-scatter.67.cloned.1.call-update) | async-done | bytes 131088 | tf_op jit(solution)/shard_map/reduce_scatter | solution.py:213
  835.6 18.1 %all_gather.105 = bf16[256,1024]{1,0:T(8,128)(2,1)S(1)} all-gather(bf16[64,1024]{1,0:T(8,128)(2,1)} %get-tuple-element.476), channel_id=1, replica_groups=mesh['pipe'=2,'dp'=4,'tensor'=4] {'tensor'}, dimensions={0}, use_global_device_ids=true | all-gather | bytes 655360 | tf_op jit(solution)/shard_map/all_gather | solution.py:161
  869.5 21.0 %all_gather.103 = bf16[256,1024]{1,0:T(8,128)(2,1)S(1)} all-gather(bf16[64,1024]{1,0:T(8,128)(2,1)S(1)} %get-tuple-element.372), channel_id=1, replica_groups=mesh['pipe'=2,'dp'=4,'tensor'=4] {'tensor'}, dimensions={0}, use_global_device_ids=true | all-gather | bytes 655360 | tf_op jit(solution)/shard_map/all_gather | solution.py:207
  1087.8 58.2 %all-reduce = f32[4096]{0:T(1024)S(1)} all-reduce(f32[4096]{0:T(1024)S(1)} %add_dynamic-update-slice_fusion), channel_id=36, replica_groups=mesh['pipe'=2,'dp'=4,'tensor'=4] {'dp','tensor'}, use_global_device_ids=true, to_apply=%region_143.144.clone | all-reduce | flops 4096 | bytes 32768
  1158.6 22.3 %reduce-scatter.81.cloned.1.call-done = bf16[64,1024]{1,0:T(8,128)(2,1)} async-done(((bf16[256,1024]{1,0:T(8,128)(2,1)}), bf16[64,1024]{1,0:T(8,128)(2,1)}) %reduce-scatter.81.cloned.1.call-update) | async-done | bytes 131088 | tf_op jit(solution)/shard_map/reduce_scatter | solution.py:227
  1182.8 21.0 %reduce-scatter.85.cloned.1.call-done = bf16[256,256]{1,0:T(8,128)(2,1)} async-done(((bf16[256,1024]{1,0:T(8,128)(2,1)}), bf16[256,256]{1,0:T(8,128)(2,1)}) %reduce-scatter.85.cloned.1.call-update) | async-done | bytes 131088 | tf_op jit(solution)/shard_map/reduce_scatter | solution.py:317
  1205.5 32.1 %reduce-scatter.87.cloned.1.call-done = bf16[256,1024]{1,0:T(8,128)(2,1)} async-done(((bf16[1024,1024]{1,0:T(8,128)(2,1)}), bf16[256,1024]{1,0:T(8,128)(2,1)}) %reduce-scatter.87.cloned.1.call-update) | async-done | bytes 524304 | tf_op jit(solution)/shard_map/reduce_scatter | solution.py:320
  1239.7 31.6 %reduce-scatter.89.cloned.1.call-done = bf16[1024,256]{1,0:T(8,128)(2,1)} async-done(((bf16[1024,1024]{1,0:T(8,128)(2,1)}), bf16[1024,256]{1,0:T(8,128)(2,1)}) %reduce-scatter.89.cloned.1.call-update) | async-done | bytes 524304 | tf_op jit(solution)/shard_map/reduce_scatter | solution.py:323
  1273.4 28.4 %reduce-scatter.83.cloned.1.call-done = bf16[256,3,256]{2,0,1:T(8,128)(2,1)} async-done(((bf16[1024,3,256]{2,0,1:T(8,128)(2,1)}), bf16[256,3,256]{2,0,1:T(8,128)(2,1)}) %reduce-scatter.83.cloned.1.call-update) | async-done | bytes 393232 | tf_op jit(solution)/shard_map/reduce_scatter | solution.py:314
  (1339 shorter events, 723.2 us)
Async XLA Ops:
  38.8 72.9 %all-gather.12.cloned.1.call-start = ((), (), s32[]{:S(2)}) async-start(), calls=%async_computation.60 | async-start | bytes 2621440 | tf_op jit(solution)/shard_map/all_gather | solution.py:275
  39.4 97.4 %reduce-scatter.37.cloned.1.call-start = ((), (), s32[]{:S(2)}) async-start(), calls=%async_computation.31 | async-start | bytes 655360 | tf_op jit(solution)/shard_map/reduce_scatter | solution.py:165
  114.8 66.9 %reduce-scatter.55.cloned.1.call-start = ((), (), s32[]{:S(2)}) async-start(), calls=%async_computation.40 | async-start | bytes 655360 | tf_op jit(solution)/shard_map/reduce_scatter | solution.py:213
  161.3 76.2 %reduce-scatter.39.cloned.1.call-start = ((), (), s32[]{:S(2)}) async-start(), calls=%async_computation.32 | async-start | bytes 1310720 | tf_op jit(solution)/shard_map/reduce_scatter | solution.py:157
  211.0 93.6 %reduce-scatter.41.cloned.1.call-start = ((), (), s32[]{:S(2)}) async-start(), calls=%async_computation.33 | async-start | bytes 655360 | tf_op jit(solution)/shard_map/reduce_scatter | solution.py:165
  291.5 87.1 %reduce-scatter.59.cloned.1.call-start = ((), (), s32[]{:S(2)}) async-start(), calls=%async_computation.42 | async-start | bytes 655360 | tf_op jit(solution)/shard_map/reduce_scatter | solution.py:213
  369.2 90.2 %reduce-scatter.45.cloned.1.call-start = ((), (), s32[]{:S(2)}) async-start(), calls=%async_computation.35 | async-start | bytes 655360 | tf_op jit(solution)/shard_map/reduce_scatter | solution.py:165
  432.9 65.7 %reduce-scatter.61.cloned.1.call-start = ((), (), s32[]{:S(2)}) async-start(), calls=%async_computation.43 | async-start | bytes 655360 | tf_op jit(solution)/shard_map/reduce_scatter | solution.py:227
  490.6 67.3 %reduce-scatter.63.cloned.1.call-start = ((), (), s32[]{:S(2)}) async-start(), calls=%async_computation.44 | async-start | bytes 655360 | tf_op jit(solution)/shard_map/reduce_scatter | solution.py:213
  535.6 67.4 %reduce-scatter.49.cloned.1.call-start = ((), (), s32[]{:S(2)}) async-start(), calls=%async_computation.37 | async-start | bytes 655360 | tf_op jit(solution)/shard_map/reduce_scatter | solution.py:165
  582.6 74.2 %reduce-scatter.51.cloned.1.call-start = ((), (), s32[]{:S(2)}) async-start(), calls=%async_computation.38 | async-start | bytes 1310720 | tf_op jit(solution)/shard_map/reduce_scatter | solution.py:157
  630.3 80.3 %reduce-scatter.53.cloned.1.call-start = ((), (), s32[]{:S(2)}) async-start(), calls=%async_computation.39 | async-start | bytes 655360 | tf_op jit(solution)/shard_map/reduce_scatter | solution.py:165
  738.0 68.7 %reduce-scatter.67.cloned.1.call-start = ((), (), s32[]{:S(2)}) async-start(), calls=%async_computation.46 | async-start | bytes 655360 | tf_op jit(solution)/shard_map/reduce_scatter | solution.py:213
  783.0 74.1 %reduce-scatter.69.cloned.1.call-start = ((), (), s32[]{:S(2)}) async-start(), calls=%async_computation.47 | async-start | bytes 655360 | tf_op jit(solution)/shard_map/reduce_scatter | solution.py:227
  835.0 71.3 %reduce-scatter.77.cloned.1.call-start = ((), (), s32[]{:S(2)}) async-start(), calls=%async_computation.51 | async-start | bytes 655360 | tf_op jit(solution)/shard_map/reduce_scatter | solution.py:165
  896.8 72.8 %reduce-scatter.73.cloned.1.call-start = ((), (), s32[]{:S(2)}) async-start(), calls=%async_computation.49 | async-start | bytes 655360 | tf_op jit(solution)/shard_map/reduce_scatter | solution.py:227
  949.3 71.1 %reduce-scatter.79.cloned.1.call-start = ((), (), s32[]{:S(2)}) async-start(), calls=%async_computation.52 | async-start | bytes 655360 | tf_op jit(solution)/shard_map/reduce_scatter | solution.py:213
  1000.5 146.2 %reduce-scatter.91.cloned.1.call-start = ((), (), s32[]{:S(2)}) async-start(), calls=%async_computation.61 | async-start | bytes 557056
  1043.5 113.7 %reduce-scatter.93.cloned.1.call-start = ((), (), s32[]{:S(2)}) async-start(), calls=%async_computation.62 | async-start | bytes 557056
  1046.4 134.5 %reduce-scatter.81.cloned.1.call-start = ((), (), s32[]{:S(2)}) async-start(), calls=%async_computation.53 | async-start | bytes 655360 | tf_op jit(solution)/shard_map/reduce_scatter | solution.py:227
  1047.9 155.9 %reduce-scatter.85.cloned.1.call-start = ((), (), s32[]{:S(2)}) async-start(), calls=%async_computation.55 | async-start | bytes 655360 | tf_op jit(solution)/shard_map/reduce_scatter | solution.py:317
  1055.2 182.4 %reduce-scatter.87.cloned.1.call-start = ((), (), s32[]{:S(2)}) async-start(), calls=%async_computation.56 | async-start | bytes 2621440 | tf_op jit(solution)/shard_map/reduce_scatter | solution.py:320
  1065.3 206.0 %reduce-scatter.89.cloned.1.call-start = ((), (), s32[]{:S(2)}) async-start(), calls=%async_computation.57 | async-start | bytes 2621440 | tf_op jit(solution)/shard_map/reduce_scatter | solution.py:323
  1076.8 224.9 %reduce-scatter.83.cloned.1.call-start = ((), (), s32[]{:S(2)}) async-start(), calls=%async_computation.54 | async-start | bytes 1966080 | tf_op jit(solution)/shard_map/reduce_scatter | solution.py:314
  (451 other events, 5399.8 us)
Sparse Core Ops, SparseCore 0:
  10.2 23.2 all-gather.7
  38.2 26.5 reduce-scatter.34
  66.3 21.0 all-gather.9
  88.8 22.8 all-gather.11
  114.9 21.8 reduce-scatter.36
  211.1 26.3 reduce-scatter.38
  357.6 20.9 reduce-scatter.58
  380.9 25.5 reduce-scatter.42
  433.0 22.2 reduce-scatter.44
  477.6 20.9 reduce-scatter.60
  500.7 34.0 reduce-scatter.46
  630.4 26.4 reduce-scatter.50
  683.4 21.8 reduce-scatter.52
  724.7 21.9 reduce-scatter.64
  748.9 34.5 reduce-scatter.74
  835.1 22.0 reduce-scatter.68
  865.9 25.9 reduce-scatter.76
  896.9 22.6 reduce-scatter.70
  1043.6 54.6 reduce-scatter.90
  1101.8 55.2 reduce-scatter.92
  1160.0 20.8 reduce-scatter.80
  1206.4 31.1 reduce-scatter.86
  1240.1 31.1 reduce-scatter.88
  1273.7 28.0 reduce-scatter.82
  (9 shorter events, 180.9 us)
